TPU v7x, 32 devices: a whole 2x2x4 slice. The times are simulated.
32 devices in a mesh: pipe: 4 (over x, core), expert: 8 (over z, y).
Axes of the slice: x: 2, y: 2, z: 4, core: 2. Of those that a mesh axis runs over, the one named last changes fastest.
Arguments:
- tokens: bfloat16 [1024, 6144], P('expert'), may hold values from -6 to 6
- expert_ids: int32 [1024, 2], P('expert'), may hold values from 0 to 7, as said below
- gate_weight: bfloat16 [6144, 16384], P(None, 'expert'), may hold values from -0.078125 to 0.078125
- up_weight: bfloat16 [6144, 16384], P(None, 'expert'), may hold values from -0.078125 to 0.078125
- d_hidden: bfloat16 [256, 16384], P('pipe', 'expert'), may hold values from -6 to 6
Outputs:
- hidden: bfloat16 [256, 16384], P('pipe', 'expert')
- d_tokens: float32 [1024, 6144], P('expert', 'pipe')
Inputs may be any that keep to these rules, and one draw needn't show every extreme that they name: `expert_ids`: the two ids of a token differ. Among the 128 tokens of one block at least 8 and at most 32 name expert 0, and in every draw some block has exactly 32 such tokens.
All inputs are finite; a program needn't handle non-finite values.
Results may differ from a plain program's by a relative error of at most 0.0029.
Values may be sent and summed in bfloat16 or wider, within the bound.
A program may use at most 128 MiB of HBM per device.

v0:
```python
import jax
import jax.numpy as jnp
from jax import lax
from jax.sharding import PartitionSpec as P

CAP = 32


def slot_select(expert_ids, first_slot, slot_count):
    is_named = jnp.any(expert_ids == 0, axis=1).astype(jnp.int32)
    slot_before = jnp.cumsum(is_named) - is_named
    positions = first_slot + jnp.arange(slot_count, dtype=jnp.int32)
    marked = (is_named[:, None] == 1) & (slot_before[:, None] == positions[None, :])
    return marked.astype(jnp.float32)


def body(tokens, expert_ids, gate_weight, up_weight, d_hidden):
    hidden_units = gate_weight.shape[1]
    slot_span = CAP // lax.axis_size("pipe")
    own_select = slot_select(expert_ids, lax.axis_index("pipe") * slot_span, slot_span)
    routed = jnp.einsum(
        "tj,td->jd", own_select.astype(jnp.bfloat16), tokens, preferred_element_type=jnp.float32
    ).astype(jnp.bfloat16)
    piece = lax.all_gather(routed, "expert", axis=0, tiled=True)
    gate_part = jnp.dot(piece, gate_weight, preferred_element_type=jnp.float32)
    up_part = jnp.dot(piece, up_weight, preferred_element_type=jnp.float32)
    joined = jnp.concatenate([gate_part, up_part], axis=1)
    gate_value = joined[:, :hidden_units]
    up_value = joined[:, hidden_units:]
    sigmoid_gate = jax.nn.sigmoid(gate_value)
    activated = gate_value * sigmoid_gate
    hidden = (activated * up_value).astype(jnp.bfloat16)
    upstream = d_hidden.astype(jnp.float32)
    d_gate = (
        upstream * up_value * sigmoid_gate * (1.0 + gate_value * (1.0 - sigmoid_gate))
    ).astype(jnp.bfloat16)
    d_up = (upstream * activated).astype(jnp.bfloat16)
    result = jnp.einsum("nh,dh->nd", d_gate, gate_weight, preferred_element_type=jnp.float32)
    slot_grads = lax.psum_scatter(
        result + jnp.einsum("nh,dh->nd", d_up, up_weight, preferred_element_type=jnp.float32),
        "expert",
        scatter_dimension=0,
        tiled=True,
    )
    pieces = lax.all_to_all(slot_grads, "pipe", split_axis=1, concat_axis=0, tiled=True)
    full_select = slot_select(expert_ids, 0, CAP)
    d_tokens = jnp.einsum("tc,cd->td", full_select, pieces, precision=lax.Precision.HIGHEST)
    return (hidden, d_tokens)


def solution(mesh):
    in_specs = (
        P("expert", None),
        P("expert", None),
        P(None, "expert"),
        P(None, "expert"),
        P("pipe", "expert"),
    )
    out_specs = (P("pipe", "expert"), P("expert", "pipe"))
    return jax.shard_map(body, mesh=mesh, in_specs=in_specs, out_specs=out_specs, check_vma=False)
```

profile of v0, /device:TPU:0, one launch (start us, length us, event | category | flops | bytes accessed | tf_op | source)
XLA Modules:
  0.0 175.9 jit_solution(8886105624319551645)
XLA Ops:
  7.2 0.0 copy-start
  7.2 0.0 reduce-scatter.2.cloned.1.call-start
  7.2 0.8 compare_reduce_fusion
  8.1 0.1 copy.9
  8.2 0.2 reduce-window.8
  8.3 0.1 reduce
  8.5 0.1 copy-done
  8.6 0.4 convolution_convert_fusion
  8.9 33.9 %all_gather.3 = bf16[64,6144]{1,0:T(8,128)(2,1)S(1)} all-gather(bf16[8,6144]{1,0:T(8,128)(2,1)S(1)} %convolution_convert_fusion), channel_id=1, replica_groups=mesh['pipe'=4,'expert'=8] {'expert'}, dimensions={0}, use_global_device_ids=true | all-gather | bytes 884736 | tf_op jit(solution)/shard_map/all_gather | solution.py:24
  42.8 0.0 copy-start.1
  42.8 10.5 %fusion.21 = f32[64,2048]{1,0:T(8,128)S(1)} fusion(bf16[64,6144]{1,0:T(8,128)(2,1)S(1)} %all_gather.3, bf16[6144,2048]{1,0:T(8,128)(2,1)} %param.7), kind=kOutput, calls=%fused_computation.30 | convolution fusion | flops 1610612736 | bytes 26476544 | tf_op jit(solution)/shard_map/dot_general | solution.py:25
  53.4 11.3 %multiply_convert_fusion = (bf16[64,2048]{1,0:T(8,128)(2,1)}, f32[64,2048]{1,0:T(8,128)S(1)}) fusion(f32[64,2048]{1,0:T(8,128)S(1)} %fusion.21, bf16[64,6144]{1,0:T(8,128)(2,1)S(1)} %all_gather.3, bf16[6144,2048]{1,0:T(8,128)(2,1)} %param.8), kind=kOutput, calls=%fused_computation.8 | convolution fusion | flops 1611399168 | bytes 27262976 | tf_op jit(solution)/shard_map/dot_general | solution.py:26
  64.7 0.0 copy-done.1
  64.7 13.6 %fusion.6 = f32[64,6144]{1,0:T(8,128)} fusion(bf16[6144,2048]{1,0:T(8,128)(2,1)} %param.7, f32[64,2048]{1,0:T(8,128)S(1)} %get-tuple-element.5, bf16[64,2048]{1,0:T(8,128)(2,1)S(1)} %copy-done.1, f32[64,2048]{1,0:T(8,128)S(1)} %fusion.21), kind=kOutput, calls=%fused_computation.11 | convolution fusion | flops 1612054528 | bytes 28049408 | tf_op jit(solution)/shard_map/nh,dh->nd/dot_general | solution.py:38
  78.3 14.2 %convolution_add_fusion = f32[64,6144]{1,0:T(8,128)} fusion(f32[64,6144]{1,0:T(8,128)} %fusion.6, bf16[6144,2048]{1,0:T(8,128)(2,1)} %param.8, bf16[64,2048]{1,0:T(8,128)(2,1)S(1)} %copy-done.1, f32[64,2048]{1,0:T(8,128)S(1)} %fusion.21), kind=kOutput, calls=%fused_computation | convolution fusion | flops 1611923456 | bytes 29097984 | tf_op jit(solution)/shard_map/nh,dh->nd/dot_general | solution.py:40
  92.4 0.0 reduce-scatter.2.cloned.1.call-update
  92.5 66.6 %reduce-scatter.2.cloned.1.call-done = f32[8,6144]{1,0:T(8,128)} async-done(((f32[64,6144]{1,0:T(8,128)}), f32[8,6144]{1,0:T(8,128)}) %reduce-scatter.2.cloned.1.call-update) | async-done | bytes 196624 | tf_op jit(solution)/shard_map/reduce_scatter | solution.py:39
  159.0 8.6 %all_to_all.19 = f32[8,4,1536]{2,0,1:T(8,128)S(1)} all-to-all(f32[8,4,1536]{2,0,1:T(8,128)} %bitcast.15), channel_id=1, replica_groups=mesh['pipe'=4,'expert'=8] {'pipe'}, dimensions={1} | all-to-all | bytes 393216 | tf_op jit(solution)/shard_map/all_to_all | solution.py:45
  167.7 1.4 fusion.9
  (3 shorter events, 0.0 us)
Async XLA Ops:
  7.2 1.4 copy-start
  7.2 151.9 %reduce-scatter.2.cloned.1.call-start = ((), (), s32[]{:S(2)}) async-start(), calls=%async_computation.2 | async-start | bytes 1769472 | tf_op jit(solution)/shard_map/reduce_scatter | solution.py:39
  42.8 21.9 %copy-start.1 = (bf16[64,2048]{1,0:T(8,128)(2,1)S(1)}, bf16[64,2048]{1,0:T(8,128)(2,1)}, u32[]{:S(2)}) copy-start(bf16[64,2048]{1,0:T(8,128)(2,1)} %param.9) | copy-start | bytes 786436
Sparse Core Ops, SparseCore 0:
  92.6 66.4 reduce-scatter.1
where the time goes:
time: 176 us
  waiting for transfers between devices  66.6 us (38%)
  matrix products  51.3 us (29%)
  blocking collectives  42.5 us (24%)
  between operations  14.1 us (8%)
    reduce_scatter x1, waiting for transfers between devices, body(): lax.psum_scatter(result + jnp.einsum('nh,dh->nd', d_up, up_weight, prefer...  66.6 us
    all_gather x1, blocking collectives, body(): piece = lax.all_gather(routed, 'expert', axis=0, tiled=True)  33.9 us
    dot_general x1, matrix products, body(): jnp.einsum('nh,dh->nd', d_up, up_weight, preferred_element_type=jnp.float32)  14.2 us
    dot_general x1, matrix products, body(): jnp.einsum('nh,dh->nd', d_gate, gate_weight, preferred_element_type=jnp.f...  13.6 us
    dot_general x1, matrix products, body(): up_part = jnp.dot(piece, up_weight, preferred_element_type=jnp.float32)  11.3 us
    dot_general x1, matrix products, body(): gate_part = jnp.dot(piece, gate_weight, preferred_element_type=jnp.float32)  10.5 us
    all_to_all x1, blocking collectives, body(): lax.all_to_all(slot_grads, 'pipe', split_axis=1, concat_axis=0, tiled=True)  8.64 us
  transfers between devices with their start and end apart: 1, of which 1 were waited for; matrix products, arithmetic and copies ran while one was open for 0% of the time, Pallas kernels for 0%

commit v1 on v0

--- a/solution.py
+++ b/solution.py
@@ -1,9 +1,17 @@
+import functools
+
 import jax
 import jax.numpy as jnp
 from jax import lax
+from jax.experimental import pallas as pl
+from jax.experimental.pallas import tpu as pltpu
 from jax.sharding import PartitionSpec as P
 
 CAP = 32
+CORES = 2
+UNIT = 16
+STEPS = 4
+MESH_ID = pl.DeviceIdType.MESH
 
 
 def slot_select(expert_ids, first_slot, slot_count):
@@ -14,7 +22,7 @@
     return marked.astype(jnp.float32)
 
 
-def body(tokens, expert_ids, gate_weight, up_weight, d_hidden):
+def plain_body(tokens, expert_ids, gate_weight, up_weight, d_hidden):
     hidden_units = gate_weight.shape[1]
     slot_span = CAP // lax.axis_size("pipe")
     own_select = slot_select(expert_ids, lax.axis_index("pipe") * slot_span, slot_span)
@@ -48,6 +56,268 @@
     return (hidden, d_tokens)
 
 
+def expert_kernel(nz, ny, tok, ids, gate, up, dh, hid, dtok,
+                  tokv, own, oth, wg, wu, accg, accu, dhv, dgv, duv, hst,
+                  csend, crecv, full, keep, ysend, yrecv, zsend, zrecv, fin, xsend, xrecv,
+                  load_sem, send_sem, recv_sem):
+    pipe, expert = lax.axis_index("pipe"), lax.axis_index("expert")
+    x, c = pipe // CORES, lax.rem(pipe, CORES)
+    z, y = expert // ny, lax.rem(expert, ny)
+    half_steps = STEPS // 2
+    width = tokv.shape[2]
+    half = wg.shape[3]
+    count = tok.shape[0]
+    span = width * half_steps
+    ring = range(1, nz)
+    z_to = {d: lax.rem(z + d, nz) for d in ring}
+    z_from = {d: lax.rem(z + nz - d, nz) for d in ring}
+    core_peer = (x * CORES + 1 - c, expert)
+    x_peer = ((1 - x) * CORES + c, expert)
+    y_peer = (pipe, z * ny + 1 - y)
+    z_peer = {d: (pipe, z_to[d] * ny + y) for d in ring}
+
+    taken = [0, 0]
+
+    def load(src, dst):
+        taken[0] += 1
+        copy = pltpu.make_async_copy(src, dst, load_sem.at[taken[0] - 1])
+        copy.start()
+        return copy
+
+    def send(src, dst, device):
+        taken[1] += 1
+        index = taken[1] - 1
+        copy = pltpu.make_async_remote_copy(
+            src_ref=src, dst_ref=dst, send_sem=send_sem.at[index], recv_sem=recv_sem.at[index],
+            device_id=device, device_id_type=MESH_ID)
+        copy.start()
+        sent.append(copy)
+        return copy
+
+    sent = []
+
+    def offset(other, s):
+        part = c if other == 0 else 1 - c
+        where = 1 - x if s < half_steps else x
+        return pl.multiple_of((where * CORES + part) * span + (s % half_steps) * width, 128)
+
+    barrier = pltpu.get_barrier_semaphore()
+    peers = [core_peer, x_peer, y_peer] + [z_peer[d] for d in ring]
+    for peer in peers:
+        pl.semaphore_signal(barrier, inc=1, device_id=peer, device_id_type=MESH_ID)
+
+    mine = pl.ds(pl.multiple_of(c * half, 128), half)
+    others = pl.ds(pl.multiple_of((1 - c) * half, 128), half)
+    tok_loads = [load(tok.at[:, pl.ds(offset(0, s), width)], tokv.at[s]) for s in range(STEPS)]
+    w_loads = {}
+    for s in range(STEPS):
+        for other in (0, 1):
+            rows = pl.ds(offset(other, s), width)
+            w_loads[other, s] = (
+                load(gate.at[rows, mine], wg.at[other, s]), load(up.at[rows, mine], wu.at[other, s]))
+    dh_load = load(dh.at[:, mine], dhv.at[c])
+
+    named_col = jnp.where((ids[:, 0:1] == 0) | (ids[:, 1:2] == 0), 1.0, 0.0)
+    row_id = lax.broadcasted_iota(jnp.int32, (count, count), 0)
+    col_id = lax.broadcasted_iota(jnp.int32, (count, count), 1)
+    spread = jnp.broadcast_to(named_col, (count, count))
+    before_row = jnp.sum(jnp.where(row_id < col_id, spread, 0.0), axis=0, keepdims=True)
+    named_row = jnp.sum(jnp.where(row_id == col_id, spread, 0.0), axis=0, keepdims=True)
+    slot_id = (lax.broadcasted_iota(jnp.int32, (UNIT, count), 0) + x * UNIT).astype(jnp.float32)
+    select = jnp.where((before_row == slot_id) & (named_row == 1.0), 1.0, 0.0).astype(jnp.bfloat16)
+
+    pl.semaphore_wait(barrier, len(peers))
+    dh_copy = send(dh.at[:, others], dhv.at[c], core_peer)
+
+    z_copies, y_copies, core_copies = {}, {}, {}
+    for s in range(STEPS):
+        tok_loads[s].wait()
+        own[s, expert] = jnp.dot(
+            select, tokv[s], preferred_element_type=jnp.float32).astype(jnp.bfloat16)
+        for d in ring:
+            z_copies[s, d] = send(own.at[s, expert], own.at[s, expert], z_peer[d])
+        y_copies[s, 0] = send(own.at[s, expert], own.at[s, expert], y_peer)
+
+    def forward(other, s):
+        block = (own if other == 0 else oth)[s].reshape(nz * ny * UNIT, width)
+        for copy in w_loads[other, s]:
+            copy.wait()
+        for acc, weight in ((accg, wg), (accu, wu)):
+            term = jnp.dot(block, weight[other, s], preferred_element_type=jnp.float32)
+            if other == 0 and s == 0:
+                acc[...] = term
+            else:
+                acc[...] += term
+
+    for i in range(STEPS + 2):
+        if i < STEPS:
+            for d in ring:
+                z_copies[i, d].wait_recv()
+                place = z_from[d] * ny + y
+                y_copies[i, d] = send(own.at[i, place], own.at[i, place], y_peer)
+        s = i - 1
+        if 0 <= s < STEPS:
+            for d in range(nz):
+                y_copies[s, d].wait_recv()
+            core_copies[s] = send(own.at[s], oth.at[s], core_peer)
+            forward(0, s)
+        s = i - 2
+        if 0 <= s < STEPS:
+            core_copies[s].wait_recv()
+            forward(1, s)
+
+    dh_load.wait()
+    dh_copy.wait_recv()
+    blocks = nz * ny
+    tile = 256 if half % 256 == 0 else half
+    for n in range(0, half, tile):
+        cols = slice(n, n + tile)
+        gate_value, up_value = accg[:, cols], accu[:, cols]
+        first = dhv[0, :, cols].astype(jnp.float32).reshape(blocks, UNIT // 2, tile)
+        second = dhv[1, :, cols].astype(jnp.float32).reshape(blocks, UNIT // 2, tile)
+        upstream = jnp.stack([first, second], axis=1).reshape(blocks * UNIT, tile)
+        sigmoid_gate = jax.nn.sigmoid(gate_value)
+        activated = gate_value * sigmoid_gate
+        hidden = (activated * up_value).reshape(blocks, 2, UNIT // 2, tile)
+        for q in (0, 1):
+            hst[q, :, cols] = hidden[:, q].reshape(blocks * UNIT // 2, tile).astype(jnp.bfloat16)
+        dgv[:, cols] = (
+            upstream * up_value * sigmoid_gate * (1.0 + gate_value * (1.0 - sigmoid_gate))
+        ).astype(jnp.bfloat16)
+        duv[:, cols] = (upstream * activated).astype(jnp.bfloat16)
+    hid_load = load(hst.at[c], hid.at[:, mine])
+
+    contract = (((1,), (1,)), ((), ()))
+
+    def backward(other, s):
+        return lax.dot_general(
+            dgv[...], wg[other, s], contract, preferred_element_type=jnp.float32
+        ) + lax.dot_general(
+            duv[...], wu[other, s], contract, preferred_element_type=jnp.float32)
+
+    core_sums, y_sums, z_sums, x_sums = {}, {}, {}, {}
+    hid_copy = None
+    for i in range(STEPS + 3):
+        if i < STEPS:
+            csend[i] = backward(1, i).astype(jnp.bfloat16)
+            core_sums[i] = send(csend.at[i], crecv.at[i], core_peer)
+            full[i % 2] = backward(0, i).reshape(blocks, UNIT, width)
+        s = i - 1
+        if 0 <= s < STEPS:
+            core_sums[s].wait_recv()
+            total = crecv[s].astype(jnp.float32).reshape(blocks, UNIT, width)
+            full[s % 2] = full[s % 2] + total
+            for k in range(nz):
+                ysend[s, k] = full[s % 2, k * ny + 1 - y].astype(jnp.bfloat16)
+                keep[s, k] = full[s % 2, k * ny + y]
+            y_sums[s] = send(ysend.at[s], yrecv.at[s], y_peer)
+            if hid_copy is None:
+                hid_copy = send(hst.at[1 - c], hid.at[:, mine], core_peer)
+        s = i - 2
+        if 0 <= s < STEPS:
+            y_sums[s].wait_recv()
+            for d in ring:
+                zsend[s, d - 1] = (
+                    keep[s, z_to[d]] + yrecv[s, z_to[d]].astype(jnp.float32)).astype(jnp.bfloat16)
+                z_sums[s, d] = send(zsend.at[s, d - 1], zrecv.at[s, d - 1], z_peer[d])
+            fin[s] = keep[s, z] + yrecv[s, z].astype(jnp.float32)
+        s = i - 3
+        if 0 <= s < STEPS:
+            for d in ring:
+                z_sums[s, d].wait_recv()
+            done = fin[s]
+            for d in ring:
+                done = done + zrecv[s, d - 1].astype(jnp.float32)
+            if s < half_steps:
+                xsend[s] = done
+                x_sums[s] = send(xsend.at[s], xrecv.at[s], x_peer)
+            else:
+                fin[s] = done
+
+    lane_sum = functools.partial(jnp.sum, axis=1, keepdims=True)
+    before_col = lane_sum(jnp.where(col_id < row_id, jnp.broadcast_to(named_row, (count, count)), 0.0))
+    lane = lax.broadcasted_iota(jnp.int32, (count, 2 * UNIT), 1)
+    position = jnp.where(lane < UNIT, lane + x * UNIT, lane - UNIT + (1 - x) * UNIT)
+    placed = jnp.where(
+        (before_col == position.astype(jnp.float32)) & (named_col == 1.0), 1.0, 0.0)
+    for s in range(half_steps):
+        x_sums[s].wait_recv()
+        slots = jnp.concatenate([fin[half_steps + s], xrecv[s]], axis=0)
+        dtok[:, s * width:(s + 1) * width] = jnp.dot(
+            placed, slots, precision=lax.Precision.HIGHEST, preferred_element_type=jnp.float32)
+
+    hid_load.wait()
+    hid_copy.wait_recv()
+    for copy in sent:
+        copy.wait_send()
+
+
+def fused_body(nz, ny, tokens, expert_ids, gate_weight, up_weight, d_hidden):
+    count, features = tokens.shape
+    hidden_units = gate_weight.shape[1]
+    rows = d_hidden.shape[0]
+    width = features // (CORES * STEPS)
+    half = hidden_units // CORES
+    blocks = nz * ny
+    half_steps = STEPS // 2
+    bf, f32 = jnp.bfloat16, jnp.float32
+    loads = STEPS * 5 + 2
+    sends = 2 + STEPS * (nz - 1 + nz + 1) + STEPS * (2 + nz - 1) + half_steps
+    hbm = pl.BlockSpec(memory_space=pl.ANY)
+    vmem = pl.BlockSpec(memory_space=pltpu.VMEM)
+    flops = 8 * blocks * UNIT * features * half
+    hidden, d_tokens = pl.pallas_call(
+        functools.partial(expert_kernel, nz, ny),
+        out_shape=(
+            jax.ShapeDtypeStruct((rows, hidden_units), bf),
+            jax.ShapeDtypeStruct((count, half_steps * width), f32),
+        ),
+        in_specs=[hbm, vmem, hbm, hbm, hbm],
+        out_specs=(hbm, vmem),
+        scratch_shapes=[
+            pltpu.VMEM((STEPS, count, width), bf),
+            pltpu.VMEM((STEPS, blocks, UNIT, width), bf),
+            pltpu.VMEM((STEPS, blocks, UNIT, width), bf),
+            pltpu.VMEM((2, STEPS, width, half), bf),
+            pltpu.VMEM((2, STEPS, width, half), bf),
+            pltpu.VMEM((blocks * UNIT, half), f32),
+            pltpu.VMEM((blocks * UNIT, half), f32),
+            pltpu.VMEM((2, rows, half), bf),
+            pltpu.VMEM((blocks * UNIT, half), bf),
+            pltpu.VMEM((blocks * UNIT, half), bf),
+            pltpu.VMEM((2, rows, half), bf),
+            pltpu.VMEM((STEPS, blocks * UNIT, width), bf),
+            pltpu.VMEM((STEPS, blocks * UNIT, width), bf),
+            pltpu.VMEM((2, blocks, UNIT, width), f32),
+            pltpu.VMEM((STEPS, nz, UNIT, width), f32),
+            pltpu.VMEM((STEPS, nz, UNIT, width), bf),
+            pltpu.VMEM((STEPS, nz, UNIT, width), bf),
+            pltpu.VMEM((STEPS, nz - 1, UNIT, width), bf),
+            pltpu.VMEM((STEPS, nz - 1, UNIT, width), bf),
+            pltpu.VMEM((STEPS, UNIT, width), f32),
+            pltpu.VMEM((half_steps, UNIT, width), f32),
+            pltpu.VMEM((half_steps, UNIT, width), f32),
+            pltpu.SemaphoreType.DMA((loads,)),
+            pltpu.SemaphoreType.DMA((sends,)),
+            pltpu.SemaphoreType.DMA((sends,)),
+        ],
+        compiler_params=pltpu.CompilerParams(
+            collective_id=0, has_side_effects=True, vmem_limit_bytes=56 * 1024 * 1024),
+        cost_estimate=pl.CostEstimate(
+            flops=flops, bytes_accessed=4 * features * half, transcendentals=0),
+    )(tokens, expert_ids, gate_weight, up_weight, d_hidden)
+    return hidden, d_tokens
+
+
+def split_of(mesh):
+    line = mesh.devices.reshape(mesh.shape["pipe"], mesh.shape["expert"])[0]
+    coords = [getattr(device, "coords", None) for device in line]
+    if coords[0] is None:
+        return len(line) // 2, 2
+    ny = len({tuple(at)[1] for at in coords})
+    return len(line) // ny, ny
+
+
 def solution(mesh):
     in_specs = (
         P("expert", None),
@@ -57,4 +327,7 @@
         P("pipe", "expert"),
     )
     out_specs = (P("pipe", "expert"), P("expert", "pipe"))
+    nz, ny = split_of(mesh)
+    fits = ny == 2 and nz > 1 and mesh.shape["pipe"] == 2 * CORES and 2 * UNIT == CAP
+    body = functools.partial(fused_body, nz, ny) if fits else plain_body
     return jax.shard_map(body, mesh=mesh, in_specs=in_specs, out_specs=out_specs, check_vma=False)

time: 176 us -> 55.4 us (0.31)
  waiting for transfers between devices: 66.6 us -> 0 us
  matrix products: 51.3 us -> 0 us
  Pallas kernels: 0 us -> 49.4 us
  blocking collectives: 42.5 us -> 0 us
  between operations: 14.1 us -> 0.64 us
  local copies, waits for them, and re-layouts: 0.26 us -> 5.15 us
    reduce_scatter x1 -> x0, waiting for transfers between devices: 66.6 us -> none  [body(): lax.psum_scatter(result + jnp.einsum('nh,dh->nd', d_up, up_weight, prefer...]
    dot_general x6 -> x0, matrix products: 51.3 us -> none  [the longest x1 14.2 us: body(): jnp.einsum('nh,dh->nd', d_up, up_weight, preferred_element_type=jnp.float32)]
    pallas_call x0 -> x1, Pallas kernels: none -> 49.4 us  [fused_body(): pl.pallas_call(functools.partial(expert_kernel, nz, ny), out_shape=(jax.S...]
    all_gather x1 -> x0, blocking collectives: 33.9 us -> none  [body(): piece = lax.all_gather(routed, 'expert', axis=0, tiled=True)]
    all_to_all x1 -> x0, blocking collectives: 8.64 us -> none  [body(): lax.all_to_all(slot_grads, 'pipe', split_axis=1, concat_axis=0, tiled=True)]
    unnamed x4 -> x3, local copies, waits for them, and re-layouts: 0.14 us -> 5.15 us
  transfers between devices with their start and end apart: 1 -> 0, of which waited for: 1 -> 0; matrix products, arithmetic and copies ran while one was open for 0% -> 0% of each run, Pallas kernels for 0% -> 0%
where the time goes in v1:
time: 55.4 us; the launch traced here: 55.2 us
  Pallas kernels  49.4 us (89%)
  local copies, waits for them, and re-layouts  5.15 us (9%)
  between operations  0.64 us (1%)
    pallas_call x1, Pallas kernels, fused_body(): pl.pallas_call(functools.partial(expert_kernel, nz, ny), out_shape=(jax.S...  49.4 us
    unnamed x3, local copies, waits for them, and re-layouts  5.15 us

profile of v1, /device:TPU:0, one launch (start us, length us, event | category | flops | bytes accessed | tf_op | source)
XLA Modules:
  0.0 55.2 jit_solution(2957891840296822250)
XLA Ops:
  0.6 1.4 %copy.7.ids = s32[128,2]{1,0:T(8,128)} copy(s32[128,2]{0,1:T(2,128)} %param.6) | data formatting | bytes 2048 | tf_op args[1]
  2.0 49.4 %shard_map.68 = (bf16[64,2048]{1,0:T(8,128)(2,1)}, f32[128,1536]{1,0:T(8,128)}) custom-call(bf16[128,6144]{1,0:T(8,128)(2,1)} %tok.1, s32[128,2]{1,0:T(8,128)} %copy.7.ids, bf16[6144,2048]{1,0:T(8,128)(2,1)} %gate.1, bf16[6144,2048]{1,0:T(8,128)(2,1)} %up.1, bf16[64,2048]{1,0:T(8,128)(2,1)} %dh.1), custom_call_target="tpu_custom_call" | custom-call | flops 6442450944 | bytes 25165824 | tf_op jit(solution)/shard_map/pallas_call | solution.py:269
  51.4 1.7 %copy.10 = bf16[64,2048]{1,0:T(8,128)(2,1)} copy(bf16[64,2048]{1,0:T(8,128)(2,1)} %get-tuple-element.4) | data formatting | bytes 524288
  53.1 2.1 %copy.11 = f32[128,1536]{1,0:T(8,128)} copy(f32[128,1536]{1,0:T(8,128)} %get-tuple-element.5) | data formatting | bytes 1572864

commit v2 on v1

--- a/solution.py
+++ b/solution.py
@@ -10,7 +10,9 @@
 CAP = 32
 CORES = 2
 UNIT = 16
-STEPS = 4
+STEPS = 6
+Y_LAG, C_LAG = 2, 3
+ADD_LAG, Y_SUM_LAG, Z_SUM_LAG = 1, 3, 5
 MESH_ID = pl.DeviceIdType.MESH
 
 
@@ -56,7 +58,30 @@
     return (hidden, d_tokens)
 
 
-def expert_kernel(nz, ny, tok, ids, gate, up, dh, hid, dtok,
+def named_counts(ids, count):
+    row_id = lax.broadcasted_iota(jnp.int32, (count, count), 0)
+    col_id = lax.broadcasted_iota(jnp.int32, (count, count), 1)
+    named_row = jnp.where((ids[0:1, :] == 0) | (ids[1:2, :] == 0), 1.0, 0.0)
+    across = jnp.broadcast_to(named_row, (count, count))
+    named_col = jnp.sum(jnp.where(row_id == col_id, across, 0.0), axis=1, keepdims=True)
+    before_col = jnp.sum(jnp.where(col_id < row_id, across, 0.0), axis=1, keepdims=True)
+    down = jnp.broadcast_to(named_col, (count, count))
+    before_row = jnp.sum(jnp.where(row_id < col_id, down, 0.0), axis=0, keepdims=True)
+    return named_row, before_row, named_col, before_col
+
+
+def place_kernel(ids, slots, hid_in, dtok, hid_out):
+    count = dtok.shape[0]
+    hid_out[...] = hid_in[...]
+    _, _, named_col, before_col = named_counts(ids, count)
+    lane = lax.broadcasted_iota(jnp.int32, (count, 2 * UNIT), 1).astype(jnp.float32)
+    placed = jnp.where((before_col == lane) & (named_col == 1.0), 1.0, 0.0)
+    dtok[...] = jnp.dot(
+        placed, slots[...].reshape(2 * UNIT, dtok.shape[1]),
+        precision=lax.Precision.HIGHEST, preferred_element_type=jnp.float32)
+
+
+def expert_kernel(nz, ny, tok, ids, gate, up, dh, hid, slots,
                   tokv, own, oth, wg, wu, accg, accu, dhv, dgv, duv, hst,
                   csend, crecv, full, keep, ysend, yrecv, zsend, zrecv, fin, xsend, xrecv,
                   load_sem, send_sem, recv_sem):
@@ -117,12 +142,7 @@
                 load(gate.at[rows, mine], wg.at[other, s]), load(up.at[rows, mine], wu.at[other, s]))
     dh_load = load(dh.at[:, mine], dhv.at[c])
 
-    named_col = jnp.where((ids[:, 0:1] == 0) | (ids[:, 1:2] == 0), 1.0, 0.0)
-    row_id = lax.broadcasted_iota(jnp.int32, (count, count), 0)
-    col_id = lax.broadcasted_iota(jnp.int32, (count, count), 1)
-    spread = jnp.broadcast_to(named_col, (count, count))
-    before_row = jnp.sum(jnp.where(row_id < col_id, spread, 0.0), axis=0, keepdims=True)
-    named_row = jnp.sum(jnp.where(row_id == col_id, spread, 0.0), axis=0, keepdims=True)
+    named_row, before_row, _, _ = named_counts(ids, count)
     slot_id = (lax.broadcasted_iota(jnp.int32, (UNIT, count), 0) + x * UNIT).astype(jnp.float32)
     select = jnp.where((before_row == slot_id) & (named_row == 1.0), 1.0, 0.0).astype(jnp.bfloat16)
 
@@ -149,19 +169,19 @@
             else:
                 acc[...] += term
 
-    for i in range(STEPS + 2):
+    for i in range(STEPS + C_LAG):
         if i < STEPS:
             for d in ring:
                 z_copies[i, d].wait_recv()
                 place = z_from[d] * ny + y
                 y_copies[i, d] = send(own.at[i, place], own.at[i, place], y_peer)
-        s = i - 1
+        s = i - Y_LAG
         if 0 <= s < STEPS:
             for d in range(nz):
                 y_copies[s, d].wait_recv()
             core_copies[s] = send(own.at[s], oth.at[s], core_peer)
             forward(0, s)
-        s = i - 2
+        s = i - C_LAG
         if 0 <= s < STEPS:
             core_copies[s].wait_recv()
             forward(1, s)
@@ -197,12 +217,11 @@
 
     core_sums, y_sums, z_sums, x_sums = {}, {}, {}, {}
     hid_copy = None
-    for i in range(STEPS + 3):
+    for i in range(STEPS + Z_SUM_LAG):
         if i < STEPS:
             csend[i] = backward(1, i).astype(jnp.bfloat16)
             core_sums[i] = send(csend.at[i], crecv.at[i], core_peer)
-            full[i % 2] = backward(0, i).reshape(blocks, UNIT, width)
-        s = i - 1
+        s = i - ADD_LAG
         if 0 <= s < STEPS:
             core_sums[s].wait_recv()
             total = crecv[s].astype(jnp.float32).reshape(blocks, UNIT, width)
@@ -213,7 +232,9 @@
             y_sums[s] = send(ysend.at[s], yrecv.at[s], y_peer)
             if hid_copy is None:
                 hid_copy = send(hst.at[1 - c], hid.at[:, mine], core_peer)
-        s = i - 2
+        if i < STEPS:
+            full[i % 2] = backward(0, i).reshape(blocks, UNIT, width)
+        s = i - Y_SUM_LAG
         if 0 <= s < STEPS:
             y_sums[s].wait_recv()
             for d in ring:
@@ -221,7 +242,7 @@
                     keep[s, z_to[d]] + yrecv[s, z_to[d]].astype(jnp.float32)).astype(jnp.bfloat16)
                 z_sums[s, d] = send(zsend.at[s, d - 1], zrecv.at[s, d - 1], z_peer[d])
             fin[s] = keep[s, z] + yrecv[s, z].astype(jnp.float32)
-        s = i - 3
+        s = i - Z_SUM_LAG
         if 0 <= s < STEPS:
             for d in ring:
                 z_sums[s, d].wait_recv()
@@ -234,17 +255,11 @@
             else:
                 fin[s] = done
 
-    lane_sum = functools.partial(jnp.sum, axis=1, keepdims=True)
-    before_col = lane_sum(jnp.where(col_id < row_id, jnp.broadcast_to(named_row, (count, count)), 0.0))
-    lane = lax.broadcasted_iota(jnp.int32, (count, 2 * UNIT), 1)
-    position = jnp.where(lane < UNIT, lane + x * UNIT, lane - UNIT + (1 - x) * UNIT)
-    placed = jnp.where(
-        (before_col == position.astype(jnp.float32)) & (named_col == 1.0), 1.0, 0.0)
     for s in range(half_steps):
+        cols = slice(s * width, (s + 1) * width)
+        slots[x, :, cols] = fin[half_steps + s]
         x_sums[s].wait_recv()
-        slots = jnp.concatenate([fin[half_steps + s], xrecv[s]], axis=0)
-        dtok[:, s * width:(s + 1) * width] = jnp.dot(
-            placed, slots, precision=lax.Precision.HIGHEST, preferred_element_type=jnp.float32)
+        slots[1 - x, :, cols] = xrecv[s]
 
     hid_load.wait()
     hid_copy.wait_recv()
@@ -266,11 +281,12 @@
     hbm = pl.BlockSpec(memory_space=pl.ANY)
     vmem = pl.BlockSpec(memory_space=pltpu.VMEM)
     flops = 8 * blocks * UNIT * features * half
-    hidden, d_tokens = pl.pallas_call(
+    ids = expert_ids.T
+    staged, slots = pl.pallas_call(
         functools.partial(expert_kernel, nz, ny),
         out_shape=(
             jax.ShapeDtypeStruct((rows, hidden_units), bf),
-            jax.ShapeDtypeStruct((count, half_steps * width), f32),
+            jax.ShapeDtypeStruct((2, UNIT, half_steps * width), f32),
         ),
         in_specs=[hbm, vmem, hbm, hbm, hbm],
         out_specs=(hbm, vmem),
@@ -305,7 +321,16 @@
             collective_id=0, has_side_effects=True, vmem_limit_bytes=56 * 1024 * 1024),
         cost_estimate=pl.CostEstimate(
             flops=flops, bytes_accessed=4 * features * half, transcendentals=0),
-    )(tokens, expert_ids, gate_weight, up_weight, d_hidden)
+    )(tokens, ids, gate_weight, up_weight, d_hidden)
+    d_tokens, hidden = pl.pallas_call(
+        place_kernel,
+        out_shape=(
+            jax.ShapeDtypeStruct((count, half_steps * width), f32),
+            jax.ShapeDtypeStruct((rows, hidden_units), bf),
+        ),
+        in_specs=[vmem, vmem, vmem],
+        out_specs=(vmem, vmem),
+    )(ids, slots, staged)
     return hidden, d_tokens
 
 

time: 55.4 us -> 47.1 us (0.85)
  local copies, waits for them, and re-layouts: 5.15 us -> 0 us
  Pallas kernels: 49.4 us -> 46.3 us
    pallas_call x1, Pallas kernels: 49.4 us -> 43.5 us  [fused_body(): pl.pallas_call(functools.partial(expert_kernel, nz, ny), out_shape=(jax.S...]
    unnamed x3 -> x0, local copies, waits for them, and re-layouts: 5.15 us -> none
    pallas_call x0 -> x1, Pallas kernels: none -> 2.79 us  [fused_body(): pl.pallas_call(place_kernel, out_shape=(jax.ShapeDtypeStruct((count, half...]
where the time goes in v2:
time: 47.1 us; the launch traced here: 46.9 us
  Pallas kernels  46.3 us (98%)
  between operations  0.64 us (1%)
    pallas_call x1, Pallas kernels, fused_body(): pl.pallas_call(functools.partial(expert_kernel, nz, ny), out_shape=(jax.S...  43.5 us
    pallas_call x1, Pallas kernels, fused_body(): pl.pallas_call(place_kernel, out_shape=(jax.ShapeDtypeStruct((count, half...  2.79 us

profile of v2, /device:TPU:0, one launch (start us, length us, event | category | flops | bytes accessed | tf_op | source)
XLA Modules:
  0.0 46.9 jit_solution(9632781942956562864)
XLA Ops:
  0.6 43.5 %shard_map.68 = (bf16[64,2048]{1,0:T(8,128)(2,1)}, f32[2,16,1536]{2,1,0:T(8,128)}) custom-call(bf16[128,6144]{1,0:T(8,128)(2,1)} %tok.1, s32[2,128]{1,0:T(2,128)} %bitcast.1, bf16[6144,2048]{1,0:T(8,128)(2,1)} %gate.1, bf16[6144,2048]{1,0:T(8,128)(2,1)} %up.1, bf16[64,2048]{1,0:T(8,128)(2,1)} %dh.1), custom_call_target="tpu_custom_call" | custom-call | flops 6442450944 | bytes 25165824 | tf_op jit(solution)/shard_map/pallas_call | solution.py:285
  44.1 2.8 %shard_map.69 = (f32[128,1536]{1,0:T(8,128)}, bf16[64,2048]{1,0:T(8,128)(2,1)}) custom-call(s32[2,128]{1,0:T(2,128)} %bitcast.2, f32[2,16,1536]{2,1,0:T(8,128)} %get-tuple-element.6.slots, bf16[64,2048]{1,0:T(8,128)(2,1)} %get-tuple-element.7.hid_in), custom_call_target="tpu_custom_call" | custom-call | tf_op jit(solution)/shard_map/pallas_call | solution.py:325

commit v3 on v2

--- a/solution.py
+++ b/solution.py
@@ -11,8 +11,8 @@
 CORES = 2
 UNIT = 16
 STEPS = 6
-Y_LAG, C_LAG = 2, 3
-ADD_LAG, Y_SUM_LAG, Z_SUM_LAG = 1, 3, 5
+Y_LAG, C_LAG = 3, 4
+ADD_LAG, Y_SUM_LAG, Z_SUM_LAG = 1, 3, 6
 MESH_ID = pl.DeviceIdType.MESH
 
 

time: 47.1 us -> 45 us (0.955)
  Pallas kernels: 46.3 us -> 44.2 us
    pallas_call x1, Pallas kernels: 43.5 us -> 41.4 us  [fused_body(): pl.pallas_call(functools.partial(expert_kernel, nz, ny), out_shape=(jax.S...]
where the time goes in v3:
time: 45 us; the launch traced here: 44.9 us
  Pallas kernels  44.2 us (98%)
  between operations  0.64 us (1%)
    pallas_call x1, Pallas kernels, fused_body(): pl.pallas_call(functools.partial(expert_kernel, nz, ny), out_shape=(jax.S...  41.4 us
    pallas_call x1, Pallas kernels, fused_body(): pl.pallas_call(place_kernel, out_shape=(jax.ShapeDtypeStruct((count, half...  2.79 us

profile of v3, /device:TPU:0, one launch (start us, length us, event | category | flops | bytes accessed | tf_op | source)
XLA Modules:
  0.0 44.9 jit_solution(16110182659739382007)
XLA Ops:
  0.6 41.4 %shard_map.68 = (bf16[64,2048]{1,0:T(8,128)(2,1)}, f32[2,16,1536]{2,1,0:T(8,128)}) custom-call(bf16[128,6144]{1,0:T(8,128)(2,1)} %tok.1, s32[2,128]{1,0:T(2,128)} %bitcast.1, bf16[6144,2048]{1,0:T(8,128)(2,1)} %gate.1, bf16[6144,2048]{1,0:T(8,128)(2,1)} %up.1, bf16[64,2048]{1,0:T(8,128)(2,1)} %dh.1), custom_call_target="tpu_custom_call" | custom-call | flops 6442450944 | bytes 25165824 | tf_op jit(solution)/shard_map/pallas_call | solution.py:285
  42.1 2.8 %shard_map.69 = (f32[128,1536]{1,0:T(8,128)}, bf16[64,2048]{1,0:T(8,128)(2,1)}) custom-call(s32[2,128]{1,0:T(2,128)} %bitcast.2, f32[2,16,1536]{2,1,0:T(8,128)} %get-tuple-element.6.slots, bf16[64,2048]{1,0:T(8,128)(2,1)} %get-tuple-element.7.hid_in), custom_call_target="tpu_custom_call" | custom-call | tf_op jit(solution)/shard_map/pallas_call | solution.py:325
